TPU v7x, 256 devices: a whole 4x4x8 slice. The times are simulated.
256 devices in a mesh: row: 8 (over x, core), col: 32 (over z, y).
Axes of the slice: x: 4, y: 4, z: 8, core: 2. Of those that a mesh axis runs over, the one named last changes fastest.
Arguments:
- density: bfloat16 [256, 16, 128, 128], P(('row', 'col')), as said below
- cols: int32 [256, 16], replicated, may hold values from 0 to 255, as said below
Outputs:
- new_density: float32 [256, 16, 128, 128], P(('row', 'col'))
Inputs may be any that keep to these rules, and one draw needn't show every extreme that they name: Block row b is held by the device with row index (b) // 32 and col index q = (b) % 32. cols[b, 0] = b and a row's entries are distinct. For 1 <= t <= 7, cols[b, 2t - 1] is held by a device of col index q + t and cols[b, 2t] by one of col index q - t (modulo 32); cols[b, 15] by one of col index q + 16. The pattern is symmetric with mirrored slots: if j = cols[b, s] then cols[j, s'] = b, where s' = s for s = 0 and s = 15, s' = s + 1 for odd s below 15, and s' = s - 1 for even s above 0. density[b, s] is exactly the transpose of density[cols[b, s], s'], with s' the mirrored slot.
All inputs are finite; a program needn't handle non-finite values.
Results may differ from a plain program's by a relative error of at most 0.0093.
Values may be sent and summed in bfloat16 or wider, within the bound.
No kernel may reach another device: no remote copies, remote signals or barrier semaphores. Data moves between devices by JAX's collectives and lax.ppermute only.
A program may use at most 128 MiB of HBM per device.

v0:
```python
import jax
import jax.numpy as jnp
from jax import lax
from jax.sharding import PartitionSpec as P


def shifted(value, axis, by):
    length = lax.axis_size(axis)
    return lax.ppermute(value, axis, [(i, (i + by) % length) for i in range(length)])


def slot_offsets(slot_count, grid_cols):
    offsets = [0]
    for stride in range(1, (slot_count - 2) // 2 + 1):
        offsets = offsets + [stride, -stride]
    return offsets + [grid_cols // 2]


def mirror_slots(slot_count):
    order = [0]
    for stride in range(1, (slot_count - 2) // 2 + 1):
        order = order + [2 * stride, 2 * stride - 1]
    return order + [slot_count - 1]


def per_device(density, cols):
    rows_here = density.shape[0]
    slot_count = density.shape[1]
    grid_cols = lax.axis_size("col")
    my_row = lax.axis_index("row")
    my_col = lax.axis_index("col")
    offsets = slot_offsets(slot_count, grid_cols)
    mirror = jnp.array(mirror_slots(slot_count), jnp.int32)
    shift_ids = jnp.array(offsets, jnp.int32)
    local_ids = jnp.arange(rows_here, dtype=jnp.int32)
    slot_ids = jnp.arange(slot_count, dtype=jnp.int32)
    source_col = (my_col - shift_ids) % grid_cols
    tile_rows = (my_row * grid_cols + source_col)[:, None] * rows_here + local_ids[None, :]
    left_cols = cols[tile_rows]
    targets = left_cols[slot_ids[:, None], local_ids[None, :], slot_ids[:, None]]
    target_cols = cols[targets]
    matches = left_cols[..., :, None] == target_cols[..., None, :]
    present = jnp.any(matches, axis=-1)
    found_slot = jnp.sum(jnp.where(matches, slot_ids, 0), axis=-1)
    target_rank = targets // rows_here // grid_cols * rows_here + targets % rows_here
    present_mask = present[..., None, None]
    gathered = lax.all_gather(density, "col", axis=0, tiled=True)
    left_blocks = gathered[source_col[:, None] * rows_here + local_ids[None, :]]
    column_blocks = lax.all_gather(density, "row", axis=0, tiled=True)
    right_blocks = column_blocks[target_rank[:, :, None], found_slot]
    right_blocks = jnp.where(present_mask, right_blocks, jnp.zeros((), right_blocks.dtype))
    square_tile = jnp.einsum(
        "sltab,sltcb->slac", left_blocks, right_blocks, preferred_element_type=jnp.float32
    )
    square_half = square_tile.astype(jnp.bfloat16)
    square_panel = lax.all_gather(square_half[None], "row", axis=0, tiled=True)
    inner_row = left_cols // rows_here // grid_cols
    inner_local = left_cols % rows_here
    from_square = square_panel[inner_row, mirror[found_slot], inner_local]
    from_square = jnp.where(present_mask, from_square, jnp.zeros((), from_square.dtype))
    cube_tile = jnp.einsum(
        "sltab,sltbc->slac", left_blocks, from_square, preferred_element_type=jnp.float32
    )
    new_tiles = 3.0 * square_tile - 2.0 * cube_tile
    returned_pieces = []
    for position, stride in enumerate(offsets):
        if stride == 0:
            returned_pieces.append(new_tiles[position])
        else:
            returned_pieces.append(shifted(new_tiles[position], "col", -stride))
    return jnp.stack(returned_pieces, axis=1)


def solution(mesh):
    in_specs = (P(("row", "col"), None, None, None), P())
    out_specs = P(("row", "col"), None, None, None)
    return jax.shard_map(
        per_device, mesh=mesh, in_specs=in_specs, out_specs=out_specs, check_vma=False
    )
```

profile of v0, /device:TPU:48, one launch (start us, length us, event | category | flops | bytes accessed | tf_op | source)
XLA Modules:
  0.0 314.3 jit_solution(2974334684125972960)
XLA Ops:
  6.5 0.7 all-gather.7.cloned.1.call-update
  7.3 0.7 all-gather.5.cloned.1.call-update
  8.1 0.8 copy.11
  8.9 0.7 compare_select_fusion.6
  9.6 0.6 gather_fusion.1
  10.2 0.7 gather_fusion.2
  10.9 0.6 gather_fusion.3
  11.4 0.4 fusion.20
  12.1 0.4 compare_reduce_fusion
  12.5 33.8 %all-gather.7.cloned.1.call-done = bf16[8,16,128,128]{3,2,1,0:T(8,128)(2,1)} async-done(((bf16[1,16,128,128]{3,2,1,0:T(8,128)(2,1)}), bf16[8,16,128,128]{3,2,1,0:T(8,128)(2,1)}) %all-gather.7.cloned.1.call-update) | async-done | bytes 4194320 | tf_op jit(solution)/shard_map/all_gather | solution.py:49
  46.3 12.1 %gather_fusion.4 = bf16[256,128,128]{2,1,0:T(8,128)(2,1)} fusion(bf16[8,16,128,128]{3,2,1,0:T(8,128)(2,1)} %all-gather.7.cloned.1.call-done, s32[256]{0:T(256)S(1)} %reshape.430), kind=kCustom, calls=%fused_computation.4 | custom fusion | bytes 16779264 | tf_op jit(solution)/shard_map/gather | solution.py:50
  58.4 127.8 %all-gather.5.cloned.1.call-done = bf16[32,16,128,128]{3,2,1,0:T(8,128)(2,1)} async-done(((bf16[1,16,128,128]{3,2,1,0:T(8,128)(2,1)}), bf16[32,16,128,128]{3,2,1,0:T(8,128)(2,1)}) %all-gather.5.cloned.1.call-update) | async-done | bytes 16777232 | tf_op jit(solution)/shard_map/all_gather | solution.py:47
  186.2 10.6 %gather_fusion = bf16[16,16,128,128]{3,2,1,0:T(8,128)(2,1)} fusion(bf16[32,16,128,128]{3,2,1,0:T(8,128)(2,1)} %all-gather.5.cloned.1.call-done, s32[1024]{0:T(1024)S(1)} %pad_clamp_fusion.3), kind=kCustom, calls=%fused_computation | custom fusion | bytes 16777280 | tf_op jit(solution)/shard_map/gather | solution.py:48
  196.8 9.0 %fusion.38 = (bf16[16,128,128]{2,1,0:T(8,128)(2,1)}, f32[16,128,128]{2,1,0:T(8,128)S(1)}) fusion(bf16[16,16,128,128]{3,2,1,0:T(8,128)(2,1)} %gather_fusion, bf16[16,16,128,128]{3,2,1,0:T(8,128)(2,1)} %bitcast.90, pred[16,16]{1,0:T(8,128)(4,1)S(1)} %compare_reduce_fusion), kind=kOutput, calls=%fused_computation.88 | convolution fusion | flops 1078198272 | bytes 18350336 | tf_op jit(solution)/shard_map/sltab,sltcb->slac/dot_general | solution.py:52
  205.9 1.9 gather_fusion.5
  208.0 33.0 %all-gather.9.cloned.1.call-done = bf16[128,128,128]{2,1,0:T(8,128)(2,1)} async-done(((bf16[16,128,128]{2,1,0:T(8,128)(2,1)}), bf16[128,128,128]{2,1,0:T(8,128)(2,1)}) %all-gather.9.cloned.1.call-update) | async-done | bytes 4194320 | tf_op jit(solution)/shard_map/all_gather | solution.py:56
  241.0 12.2 %gather_fusion.6 = bf16[256,128,128]{2,1,0:T(8,128)(2,1)} fusion(bf16[8,16,1,128,128]{4,3,1,0,2:T(8,128)(2,1)} %bitcast.89, s32[256]{0:T(256)S(1)} %reshape.446), kind=kCustom, calls=%fused_computation.6 | custom fusion | bytes 16780288 | tf_op jit(solution)/shard_map/gather | solution.py:59
  253.2 8.2 %fusion.17 = f32[16,128,128]{2,1,0:T(8,128)S(1)} fusion(bf16[16,16,128,128]{3,2,1,0:T(8,128)(2,1)} %gather_fusion, bf16[16,16,128,128]{3,2,1,0:T(8,128)(2,1)} %bitcast.91, pred[16,16]{1,0:T(8,128)(4,1)S(1)} %compare_reduce_fusion, f32[16,128,128]{2,1,0:T(8,128)S(1)} %get-tuple-element.23), kind=kOutput, calls=%fused_computation.18 | convolution fusion | flops 1078722560 | bytes 18874624 | tf_op jit(solution)/shard_map/sltab,sltbc->slac/dot_general | solution.py:61
  261.5 0.8 collective-permute-start
  262.3 1.5 collective-permute-start.1
  263.8 1.2 collective-permute-start.2
  265.0 3.2 %collective-permute-start.3 = (f32[1,128,128]{2,1,0:T(8,128)S(1)}, f32[1,128,128]{2,1,0:T(8,128)S(1)}, u32[]{:S(2)}, u32[]{:S(2)}) collective-permute-start(f32[1,128,128]{2,1,0:T(8,128)S(1)} %get-tuple-element.18), channel_id=1, source_target_pairs={{0,2},{1,3},{2,4},{3,5},{4,6},{5,7},{6,8},{7,9},{8,10},{9,11},{10,... | collective-permute-start | bytes 196616 | tf_op jit(solution)/shard_map/ppermute | solution.py:9
  268.3 3.2 %collective-permute-start.4 = (f32[1,128,128]{2,1,0:T(8,128)S(1)}, f32[1,128,128]{2,1,0:T(8,128)S(1)}, u32[]{:S(2)}, u32[]{:S(2)}) collective-permute-start(f32[1,128,128]{2,1,0:T(8,128)S(1)} %get-tuple-element.17), channel_id=1, source_target_pairs={{0,29},{1,30},{2,31},{3,0},{4,1},{5,2},{6,3},{7,4},{8,5},{9,6},{10... | collective-permute-start | bytes 196616 | tf_op jit(solution)/shard_map/ppermute | solution.py:9
  271.4 5.9 %collective-permute-start.6 = (f32[1,128,128]{2,1,0:T(8,128)S(1)}, f32[1,128,128]{2,1,0:T(8,128)S(1)}, u32[]{:S(2)}, u32[]{:S(2)}) collective-permute-start(f32[1,128,128]{2,1,0:T(8,128)S(1)} %get-tuple-element.15), channel_id=1, source_target_pairs={{0,28},{1,29},{2,30},{3,31},{4,0},{5,1},{6,2},{7,3},{8,4},{9,5},{1... | collective-permute-start | bytes 196616 | tf_op jit(solution)/shard_map/ppermute | solution.py:9
  277.4 3.4 %collective-permute-start.8 = (f32[1,128,128]{2,1,0:T(8,128)S(1)}, f32[1,128,128]{2,1,0:T(8,128)S(1)}, u32[]{:S(2)}, u32[]{:S(2)}) collective-permute-start(f32[1,128,128]{2,1,0:T(8,128)S(1)} %get-tuple-element.13), channel_id=1, source_target_pairs={{0,27},{1,28},{2,29},{3,30},{4,31},{5,0},{6,1},{7,2},{8,3},{9,4},{... | collective-permute-start | bytes 196616 | tf_op jit(solution)/shard_map/ppermute | solution.py:9
  281.1 3.7 %collective-permute-start.10 = (f32[1,128,128]{2,1,0:T(8,128)S(1)}, f32[1,128,128]{2,1,0:T(8,128)S(1)}, u32[]{:S(2)}, u32[]{:S(2)}) collective-permute-start(f32[1,128,128]{2,1,0:T(8,128)S(1)} %get-tuple-element.11), channel_id=1, source_target_pairs={{0,26},{1,27},{2,28},{3,29},{4,30},{5,31},{6,0},{7,1},{8,2},{9,3},... | collective-permute-start | bytes 196616 | tf_op jit(solution)/shard_map/ppermute | solution.py:9
  284.8 1.7 collective-permute-start.11
  286.6 10.8 %collective-permute-start.12 = (f32[1,128,128]{2,1,0:T(8,128)S(1)}, f32[1,128,128]{2,1,0:T(8,128)S(1)}, u32[]{:S(2)}, u32[]{:S(2)}) collective-permute-start(f32[1,128,128]{2,1,0:T(8,128)S(1)} %get-tuple-element.9), channel_id=1, source_target_pairs={{0,25},{1,26},{2,27},{3,28},{4,29},{5,30},{6,31},{7,0},{8,1},{9,2}... | collective-permute-start | bytes 196616 | tf_op jit(solution)/shard_map/ppermute | solution.py:9
  297.6 3.0 collective-permute-start.14
  300.6 5.5 %collective-permute-done.13 = f32[1,128,128]{2,1,0:T(8,128)S(1)} collective-permute-done((f32[1,128,128]{2,1,0:T(8,128)S(1)}, f32[1,128,128]{2,1,0:T(8,128)S(1)}, u32[]{:S(2)}, u32[]{:S(2)}) %collective-permute-start.13) | collective-permute-done | bytes 65568 | tf_op jit(solution)/shard_map/ppermute | solution.py:9
  306.1 1.0 copy-done.1
  307.1 0.6 bitcast_dynamic-update-slice_fusion
  (64 shorter events, 1.2 us)
Async XLA Ops:
  6.5 39.8 %all-gather.7.cloned.1.call-start = ((), (), s32[]{:S(2)}) async-start(), calls=%async_computation.1 | async-start | bytes 4718592 | tf_op jit(solution)/shard_map/all_gather | solution.py:49
  7.3 179.0 %all-gather.5.cloned.1.call-start = ((), (), s32[]{:S(2)}) async-start(), calls=%async_computation | async-start | bytes 17301504 | tf_op jit(solution)/shard_map/all_gather | solution.py:47
  8.0 233.0 %all-gather.9.cloned.1.call-start = ((), (), s32[]{:S(2)}) async-start(), calls=%async_computation.2 | async-start | bytes 4718592 | tf_op jit(solution)/shard_map/all_gather | solution.py:56
  196.8 9.1 %copy-start = (s32[16]{0:T(128)S(1)}, s32[16]{0:T(128)}, u32[]{:S(2)}) copy-start(s32[16]{0:T(128)} %constant.115.clone) | copy-start | bytes 196
  261.5 9.9 %collective-permute-start = (f32[1,128,128]{2,1,0:T(8,128)S(1)}, f32[1,128,128]{2,1,0:T(8,128)S(1)}, u32[]{:S(2)}, u32[]{:S(2)}) collective-permute-start(f32[1,128,128]{2,1,0:T(8,128)S(1)} %get-tuple-element.21), channel_id=1, source_target_pairs={{0,31},{1,0},{2,1},{3,2},{4,3},{5,4},{6,5},{7,6},{8,7},{9,8},{10,9... | collective-permute-start | bytes 196616 | tf_op jit(solution)/shard_map/ppermute | solution.py:9
  262.3 9.1 %collective-permute-start.1 = (f32[1,128,128]{2,1,0:T(8,128)S(1)}, f32[1,128,128]{2,1,0:T(8,128)S(1)}, u32[]{:S(2)}, u32[]{:S(2)}) collective-permute-start(f32[1,128,128]{2,1,0:T(8,128)S(1)} %get-tuple-element.20), channel_id=1, source_target_pairs={{0,1},{1,2},{2,3},{3,4},{4,5},{5,6},{6,7},{7,8},{8,9},{9,10},{10,1... | collective-permute-start | bytes 196616 | tf_op jit(solution)/shard_map/ppermute | solution.py:9
  263.8 13.5 %collective-permute-start.2 = (f32[1,128,128]{2,1,0:T(8,128)S(1)}, f32[1,128,128]{2,1,0:T(8,128)S(1)}, u32[]{:S(2)}, u32[]{:S(2)}) collective-permute-start(f32[1,128,128]{2,1,0:T(8,128)S(1)} %get-tuple-element.19), channel_id=1, source_target_pairs={{0,30},{1,31},{2,0},{3,1},{4,2},{5,3},{6,4},{7,5},{8,6},{9,7},{10,... | collective-permute-start | bytes 196616 | tf_op jit(solution)/shard_map/ppermute | solution.py:9
  265.0 12.4 %collective-permute-start.3 = (f32[1,128,128]{2,1,0:T(8,128)S(1)}, f32[1,128,128]{2,1,0:T(8,128)S(1)}, u32[]{:S(2)}, u32[]{:S(2)}) collective-permute-start(f32[1,128,128]{2,1,0:T(8,128)S(1)} %get-tuple-element.18), channel_id=1, source_target_pairs={{0,2},{1,3},{2,4},{3,5},{4,6},{5,7},{6,8},{7,9},{8,10},{9,11},{10,... | collective-permute-start | bytes 196616 | tf_op jit(solution)/shard_map/ppermute | solution.py:9
  268.3 12.6 %collective-permute-start.4 = (f32[1,128,128]{2,1,0:T(8,128)S(1)}, f32[1,128,128]{2,1,0:T(8,128)S(1)}, u32[]{:S(2)}, u32[]{:S(2)}) collective-permute-start(f32[1,128,128]{2,1,0:T(8,128)S(1)} %get-tuple-element.17), channel_id=1, source_target_pairs={{0,29},{1,30},{2,31},{3,0},{4,1},{5,2},{6,3},{7,4},{8,5},{9,6},{10... | collective-permute-start | bytes 196616 | tf_op jit(solution)/shard_map/ppermute | solution.py:9
  271.4 9.6 %collective-permute-start.5 = (f32[1,128,128]{2,1,0:T(8,128)S(1)}, f32[1,128,128]{2,1,0:T(8,128)S(1)}, u32[]{:S(2)}, u32[]{:S(2)}) collective-permute-start(f32[1,128,128]{2,1,0:T(8,128)S(1)} %get-tuple-element.16), channel_id=1, source_target_pairs={{0,3},{1,4},{2,5},{3,6},{4,7},{5,8},{6,9},{7,10},{8,11},{9,12},{10... | collective-permute-start | bytes 196616 | tf_op jit(solution)/shard_map/ppermute | solution.py:9
  271.4 13.4 %collective-permute-start.6 = (f32[1,128,128]{2,1,0:T(8,128)S(1)}, f32[1,128,128]{2,1,0:T(8,128)S(1)}, u32[]{:S(2)}, u32[]{:S(2)}) collective-permute-start(f32[1,128,128]{2,1,0:T(8,128)S(1)} %get-tuple-element.15), channel_id=1, source_target_pairs={{0,28},{1,29},{2,30},{3,31},{4,0},{5,1},{6,2},{7,3},{8,4},{9,5},{1... | collective-permute-start | bytes 196616 | tf_op jit(solution)/shard_map/ppermute | solution.py:9
  277.3 9.3 %collective-permute-start.7 = (f32[1,128,128]{2,1,0:T(8,128)S(1)}, f32[1,128,128]{2,1,0:T(8,128)S(1)}, u32[]{:S(2)}, u32[]{:S(2)}) collective-permute-start(f32[1,128,128]{2,1,0:T(8,128)S(1)} %get-tuple-element.14), channel_id=1, source_target_pairs={{0,4},{1,5},{2,6},{3,7},{4,8},{5,9},{6,10},{7,11},{8,12},{9,13},{1... | collective-permute-start | bytes 196616 | tf_op jit(solution)/shard_map/ppermute | solution.py:9
  277.4 20.0 %collective-permute-start.8 = (f32[1,128,128]{2,1,0:T(8,128)S(1)}, f32[1,128,128]{2,1,0:T(8,128)S(1)}, u32[]{:S(2)}, u32[]{:S(2)}) collective-permute-start(f32[1,128,128]{2,1,0:T(8,128)S(1)} %get-tuple-element.13), channel_id=1, source_target_pairs={{0,27},{1,28},{2,29},{3,30},{4,31},{5,0},{6,1},{7,2},{8,3},{9,4},{... | collective-permute-start | bytes 196616 | tf_op jit(solution)/shard_map/ppermute | solution.py:9
  280.9 16.7 %collective-permute-start.9 = (f32[1,128,128]{2,1,0:T(8,128)S(1)}, f32[1,128,128]{2,1,0:T(8,128)S(1)}, u32[]{:S(2)}, u32[]{:S(2)}) collective-permute-start(f32[1,128,128]{2,1,0:T(8,128)S(1)} %get-tuple-element.12), channel_id=1, source_target_pairs={{0,5},{1,6},{2,7},{3,8},{4,9},{5,10},{6,11},{7,12},{8,13},{9,14},{... | collective-permute-start | bytes 196616 | tf_op jit(solution)/shard_map/ppermute | solution.py:9
  281.1 19.5 %collective-permute-start.10 = (f32[1,128,128]{2,1,0:T(8,128)S(1)}, f32[1,128,128]{2,1,0:T(8,128)S(1)}, u32[]{:S(2)}, u32[]{:S(2)}) collective-permute-start(f32[1,128,128]{2,1,0:T(8,128)S(1)} %get-tuple-element.11), channel_id=1, source_target_pairs={{0,26},{1,27},{2,28},{3,29},{4,30},{5,31},{6,0},{7,1},{8,2},{9,3},... | collective-permute-start | bytes 196616 | tf_op jit(solution)/shard_map/ppermute | solution.py:9
  284.8 15.7 %collective-permute-start.11 = (f32[1,128,128]{2,1,0:T(8,128)S(1)}, f32[1,128,128]{2,1,0:T(8,128)S(1)}, u32[]{:S(2)}, u32[]{:S(2)}) collective-permute-start(f32[1,128,128]{2,1,0:T(8,128)S(1)} %get-tuple-element.10), channel_id=1, source_target_pairs={{0,6},{1,7},{2,8},{3,9},{4,10},{5,11},{6,12},{7,13},{8,14},{9,15},... | collective-permute-start | bytes 196616 | tf_op jit(solution)/shard_map/ppermute | solution.py:9
  286.6 14.0 %collective-permute-start.12 = (f32[1,128,128]{2,1,0:T(8,128)S(1)}, f32[1,128,128]{2,1,0:T(8,128)S(1)}, u32[]{:S(2)}, u32[]{:S(2)}) collective-permute-start(f32[1,128,128]{2,1,0:T(8,128)S(1)} %get-tuple-element.9), channel_id=1, source_target_pairs={{0,25},{1,26},{2,27},{3,28},{4,29},{5,30},{6,31},{7,0},{8,1},{9,2}... | collective-permute-start | bytes 196616 | tf_op jit(solution)/shard_map/ppermute | solution.py:9
  297.4 8.7 %collective-permute-start.13 = (f32[1,128,128]{2,1,0:T(8,128)S(1)}, f32[1,128,128]{2,1,0:T(8,128)S(1)}, u32[]{:S(2)}, u32[]{:S(2)}) collective-permute-start(f32[1,128,128]{2,1,0:T(8,128)S(1)} %get-tuple-element.8), channel_id=1, source_target_pairs={{0,7},{1,8},{2,9},{3,10},{4,11},{5,12},{6,13},{7,14},{8,15},{9,16}... | collective-permute-start | bytes 196616 | tf_op jit(solution)/shard_map/ppermute | solution.py:9
  297.6 8.6 %collective-permute-start.14 = (f32[1,128,128]{2,1,0:T(8,128)S(1)}, f32[1,128,128]{2,1,0:T(8,128)S(1)}, u32[]{:S(2)}, u32[]{:S(2)}) collective-permute-start(f32[1,128,128]{2,1,0:T(8,128)S(1)} %get-tuple-element.7), channel_id=1, source_target_pairs={{0,16},{1,17},{2,18},{3,19},{4,20},{5,21},{6,22},{7,23},{8,24},{9,... | collective-permute-start | bytes 196616 | tf_op jit(solution)/shard_map/ppermute | solution.py:9
  306.1 1.0 copy-start.1
Sparse Core Ops, SparseCore 0:
  9.2 37.0 all-gather.6
  48.9 137.2 all-gather.4
  205.9 35.0 all-gather.8
where the time goes:
time: 314 us
  waiting for transfers between devices  202 us (64%)
  local copies, waits for them, and re-layouts  41.5 us (13%)
  starting transfers between devices  38.9 us (12%)
  matrix products  17.2 us (5%)
  between operations  13.4 us (4%)
    all_gather x1, waiting for transfers between devices, per_device(): gathered = lax.all_gather(density, 'col', axis=0, tiled=True)  128 us
    ppermute x15, starting transfers between devices, shifted(): lax.ppermute(value, axis, [(i, (i + by) % length) for i in range(length)])  38.8 us
    all_gather x1, waiting for transfers between devices, per_device(): column_blocks = lax.all_gather(density, 'row', axis=0, tiled=True)  33.8 us
    all_gather x1, waiting for transfers between devices, per_device(): square_panel = lax.all_gather(square_half[None], 'row', axis=0, tiled=True)  33 us
    gather x3, local copies, waits for them, and re-layouts, per_device(): from_square = square_panel[inner_row, mirror[found_slot], inner_local]  14.2 us
    gather x1, local copies, waits for them, and re-layouts, per_device(): right_blocks = column_blocks[target_rank[:, :, None], found_slot]  12.1 us
    gather x1, local copies, waits for them, and re-layouts, per_device(): left_blocks = gathered[source_col[:, None] * rows_here + local_ids[None, :]]  10.6 us
    dot_general x1, matrix products, per_device(): jnp.einsum('sltab,sltcb->slac', left_blocks, right_blocks, preferred_elem...  8.99 us
  transfers between devices with their start and end apart: 18, of which 4 were waited for; matrix products, arithmetic and copies ran while one was open for 6% of the time, Pallas kernels for 0%

commit v1 on v0

--- a/solution.py
+++ b/solution.py
@@ -2,6 +2,27 @@
 import jax.numpy as jnp
 from jax import lax
 from jax.sharding import PartitionSpec as P
+
+
+def ring_gather(shard, axis, dim):
+    peers, here, rows = (lax.axis_size(axis), lax.axis_index(axis), shard.shape[dim])
+    upward = [(i, (i + 1) % peers) for i in range(peers)]
+    behind = [(i, (i - 1) % peers) for i in range(peers)]
+    out = jnp.zeros((*shard.shape[:dim], peers * rows, *shard.shape[dim + 1 :]), shard.dtype)
+    out = lax.dynamic_update_slice_in_dim(out, shard, here * rows, axis=dim)
+    from_left = from_right = shard
+    half = peers // 2
+    for step in range(1, half + 1):
+        from_left = lax.ppermute(from_left, axis, upward)
+        out = lax.dynamic_update_slice_in_dim(
+            out, from_left, (here - step) % peers * rows, axis=dim
+        )
+        if step < peers - half:
+            from_right = lax.ppermute(from_right, axis, behind)
+            out = lax.dynamic_update_slice_in_dim(
+                out, from_right, (here + step) % peers * rows, axis=dim
+            )
+    return out
 
 
 def shifted(value, axis, by):
@@ -46,7 +67,7 @@
     present_mask = present[..., None, None]
     gathered = lax.all_gather(density, "col", axis=0, tiled=True)
     left_blocks = gathered[source_col[:, None] * rows_here + local_ids[None, :]]
-    column_blocks = lax.all_gather(density, "row", axis=0, tiled=True)
+    column_blocks = ring_gather(density, "row", 0)
     right_blocks = column_blocks[target_rank[:, :, None], found_slot]
     right_blocks = jnp.where(present_mask, right_blocks, jnp.zeros((), right_blocks.dtype))
     square_tile = jnp.einsum(

time: 314 us -> 278 us (0.89)
  waiting for transfers between devices: 202 us -> 145 us
  local copies, waits for them, and re-layouts: 41.5 us -> 52.6 us
  starting transfers between devices: 38.9 us -> 47.8 us
    all_gather x1, waiting for transfers between devices: 128 us -> 89.7 us  [per_device(): gathered = lax.all_gather(density, 'col', axis=0, tiled=True)]
    all_gather x1 -> x0, waiting for transfers between devices: 33.8 us -> none  [per_device(): column_blocks = lax.all_gather(density, 'row', axis=0, tiled=True)]
    ppermute x0 -> x7, waiting for transfers between devices: none -> 16.3 us  [the longest x4 14.4 us: ring_gather(): from_left = lax.ppermute(from_left, axis, upward)]
    ppermute x0 -> x7, starting transfers between devices: none -> 8.87 us  [the longest x3 8.84 us: ring_gather(): from_right = lax.ppermute(from_right, axis, behind)]
    dynamic_update_slice x0 -> x8, local copies, waits for them, and re-layouts: none -> 7.77 us  [the longest x4 3.37 us: ring_gather(): lax.dynamic_update_slice_in_dim(out, from_left, (here - step) % peers * r...]
  transfers between devices with their start and end apart: 18 -> 24, of which waited for: 4 -> 8; matrix products, arithmetic and copies ran while one was open for 6% -> 11% of each run, Pallas kernels for 0% -> 0%
where the time goes in v1:
time: 278 us
  waiting for transfers between devices  145 us (52%)
  local copies, waits for them, and re-layouts  52.6 us (19%)
  starting transfers between devices  47.8 us (17%)
  matrix products  17.2 us (6%)
  between operations  13.7 us (5%)
    all_gather x1, waiting for transfers between devices, per_device(): gathered = lax.all_gather(density, 'col', axis=0, tiled=True)  89.7 us
    ppermute x15, starting transfers between devices, shifted(): lax.ppermute(value, axis, [(i, (i + by) % length) for i in range(length)])  38.8 us
    all_gather x1, waiting for transfers between devices, per_device(): square_panel = lax.all_gather(square_half[None], 'row', axis=0, tiled=True)  33 us
    ppermute x4, waiting for transfers between devices, ring_gather(): from_left = lax.ppermute(from_left, axis, upward)  14.4 us
    gather x3, local copies, waits for them, and re-layouts, per_device(): from_square = square_panel[inner_row, mirror[found_slot], inner_local]  14.2 us
    gather x1, local copies, waits for them, and re-layouts, per_device(): right_blocks = column_blocks[target_rank[:, :, None], found_slot]  12.3 us
    gather x1, local copies, waits for them, and re-layouts, per_device(): left_blocks = gathered[source_col[:, None] * rows_here + local_ids[None, :]]  10.6 us
    dot_general x1, matrix products, per_device(): jnp.einsum('sltab,sltcb->slac', left_blocks, right_blocks, preferred_elem...  9 us
  transfers between devices with their start and end apart: 24, of which 8 were waited for; matrix products, arithmetic and copies ran while one was open for 11% of the time, Pallas kernels for 0%

profile of v1, /device:TPU:48, one launch (start us, length us, event | category | flops | bytes accessed | tf_op | source)
XLA Modules:
  0.0 278.1 jit_solution(16338076315306530872)
XLA Ops:
  7.3 2.9 %collective-permute-start.1 = (bf16[1,16,128,128]{3,2,1,0:T(8,128)(2,1)}, bf16[1,16,128,128]{3,2,1,0:T(8,128)(2,1)S(1)}, u32[]{:S(2)}, u32[]{:S(2)}) collective-permute-start(bf16[1,16,128,128]{3,2,1,0:T(8,128)(2,1)} %param.4), channel_id=1, source_target_pairs={{0,224},{32,0},{64,32},{96,64},{128,96},{160,128},{192,160},{224,1... | collective-permute-start | bytes 1572872 | tf_op jit(solution)/shard_map/ppermute | solution.py:21
  14.1 3.3 %collective-permute-done = bf16[1,16,128,128]{3,2,1,0:T(8,128)(2,1)S(1)} collective-permute-done((bf16[1,16,128,128]{3,2,1,0:T(8,128)(2,1)}, bf16[1,16,128,128]{3,2,1,0:T(8,128)(2,1)S(1)}, u32[]{:S(2)}, u32[]{:S(2)}) %collective-permute-start) | collective-permute-done | bytes 524320 | tf_op jit(solution)/shard_map/ppermute | solution.py:16
  17.5 3.0 %collective-permute-start.3 = (bf16[1,16,128,128]{3,2,1,0:T(8,128)(2,1)S(1)}, bf16[1,16,128,128]{3,2,1,0:T(8,128)(2,1)S(1)}, u32[]{:S(2)}, u32[]{:S(2)}) collective-permute-start(bf16[1,16,128,128]{3,2,1,0:T(8,128)(2,1)S(1)} %collective-permute-done.1), channel_id=1, source_target_pairs={{0,224},{32,0},{64,32},{96,64},{128,96},{160,128},{192,160},{224,1... | collective-permute-start | bytes 1572872 | tf_op jit(solution)/shard_map/ppermute | solution.py:21
  20.4 6.7 %collective-permute-done.2 = bf16[1,16,128,128]{3,2,1,0:T(8,128)(2,1)S(1)} collective-permute-done((bf16[1,16,128,128]{3,2,1,0:T(8,128)(2,1)S(1)}, bf16[1,16,128,128]{3,2,1,0:T(8,128)(2,1)S(1)}, u32[]{:S(2)}, u32[]{:S(2)}) %collective-permute-start.2) | collective-permute-done | bytes 524320 | tf_op jit(solution)/shard_map/ppermute | solution.py:16
  27.7 3.0 %broadcast_in_dim.60 = bf16[8,16,128,128]{3,2,1,0:T(8,128)(2,1)} broadcast(bf16[]{:T(256)} %constant.149.clone.1), dimensions={} | broadcast | bytes 4194306 | tf_op jit(solution)/shard_map/broadcast_in_dim | solution.py:11
  30.7 1.9 constant_dynamic-update-slice_fusion.7
  32.6 2.9 %collective-permute-start.5 = (bf16[1,16,128,128]{3,2,1,0:T(8,128)(2,1)S(1)}, bf16[1,16,128,128]{3,2,1,0:T(8,128)(2,1)S(1)}, u32[]{:S(2)}, u32[]{:S(2)}) collective-permute-start(bf16[1,16,128,128]{3,2,1,0:T(8,128)(2,1)S(1)} %collective-permute-done.3), channel_id=1, source_target_pairs={{0,224},{32,0},{64,32},{96,64},{128,96},{160,128},{192,160},{224,1... | collective-permute-start | bytes 1572872 | tf_op jit(solution)/shard_map/ppermute | solution.py:21
  37.0 0.9 constant_dynamic-update-slice_fusion.5
  37.8 0.8 constant_dynamic-update-slice_fusion.4
  40.4 1.9 collective-permute-done.5
  43.0 3.8 %collective-permute-done.6 = bf16[1,16,128,128]{3,2,1,0:T(8,128)(2,1)S(1)} collective-permute-done((bf16[1,16,128,128]{3,2,1,0:T(8,128)(2,1)S(1)}, bf16[1,16,128,128]{3,2,1,0:T(8,128)(2,1)S(1)}, u32[]{:S(2)}, u32[]{:S(2)}) %collective-permute-start.6) | collective-permute-done | bytes 524320 | tf_op jit(solution)/shard_map/ppermute | solution.py:16
  46.8 0.9 constant_dynamic-update-slice_fusion
  47.6 12.3 %gather_fusion.4 = bf16[256,128,128]{2,1,0:T(8,128)(2,1)} fusion(bf16[8,16,128,128]{3,2,1,0:T(8,128)(2,1)} %constant_dynamic-update-slice_fusion, s32[256]{0:T(256)S(1)} %reshape.430), kind=kCustom, calls=%fused_computation.4 | custom fusion | bytes 16779264 | tf_op jit(solution)/shard_map/gather | solution.py:71
  60.0 89.7 %all-gather.4.cloned.1.call-done = bf16[32,16,128,128]{3,2,1,0:T(8,128)(2,1)} async-done(((bf16[1,16,128,128]{3,2,1,0:T(8,128)(2,1)}), bf16[32,16,128,128]{3,2,1,0:T(8,128)(2,1)}) %all-gather.4.cloned.1.call-update) | async-done | bytes 16777232 | tf_op jit(solution)/shard_map/all_gather | solution.py:68
  149.7 10.6 %gather_fusion = bf16[16,16,128,128]{3,2,1,0:T(8,128)(2,1)} fusion(bf16[32,16,128,128]{3,2,1,0:T(8,128)(2,1)} %all-gather.4.cloned.1.call-done, s32[1024]{0:T(1024)S(1)} %pad_clamp_fusion.3), kind=kCustom, calls=%fused_computation | custom fusion | bytes 16777280 | tf_op jit(solution)/shard_map/gather | solution.py:69
  160.3 9.0 %fusion.37 = (bf16[16,128,128]{2,1,0:T(8,128)(2,1)}, f32[16,128,128]{2,1,0:T(8,128)S(1)}) fusion(bf16[16,16,128,128]{3,2,1,0:T(8,128)(2,1)} %gather_fusion, bf16[16,16,128,128]{3,2,1,0:T(8,128)(2,1)} %bitcast.90, pred[16,16]{1,0:T(8,128)(4,1)S(1)} %compare_reduce_fusion), kind=kOutput, calls=%fused_computation.96 | convolution fusion | flops 1078198272 | bytes 18350336 | tf_op jit(solution)/shard_map/sltab,sltcb->slac/dot_general | solution.py:73
  169.4 1.9 gather_fusion.5
  171.5 33.0 %all-gather.6.cloned.1.call-done = bf16[128,128,128]{2,1,0:T(8,128)(2,1)} async-done(((bf16[16,128,128]{2,1,0:T(8,128)(2,1)}), bf16[128,128,128]{2,1,0:T(8,128)(2,1)}) %all-gather.6.cloned.1.call-update) | async-done | bytes 4194320 | tf_op jit(solution)/shard_map/all_gather | solution.py:77
  204.5 12.3 %gather_fusion.6 = bf16[256,128,128]{2,1,0:T(8,128)(2,1)} fusion(bf16[8,16,1,128,128]{4,3,1,0,2:T(8,128)(2,1)} %bitcast.89, s32[256]{0:T(256)S(1)} %reshape.446), kind=kCustom, calls=%fused_computation.6 | custom fusion | bytes 16780288 | tf_op jit(solution)/shard_map/gather | solution.py:80
  216.8 8.2 %multiply_subtract_fusion = f32[16,128,128]{2,1,0:T(8,128)S(1)} fusion(f32[16,128,128]{2,1,0:T(8,128)S(1)} %get-tuple-element.23, bf16[16,16,128,128]{3,2,1,0:T(8,128)(2,1)} %gather_fusion, bf16[16,16,128,128]{3,2,1,0:T(8,128)(2,1)} %bitcast.91, pred[16,16]{1,0:T(8,128)(4,1)S(1)} %compare_reduce_fusion), kind=kOutput, calls=%fused_computation.18 | convolution fusion | flops 1078722560 | bytes 18874624 | tf_op jit(solution)/shard_map/sltab,sltbc->slac/dot_general | solution.py:82
  225.9 1.5 collective-permute-start.8
  227.4 1.2 collective-permute-start.9
  228.6 3.3 %collective-permute-start.10 = (f32[1,128,128]{2,1,0:T(8,128)S(1)}, f32[1,128,128]{2,1,0:T(8,128)S(1)}, u32[]{:S(2)}, u32[]{:S(2)}) collective-permute-start(f32[1,128,128]{2,1,0:T(8,128)S(1)} %get-tuple-element.18), channel_id=1, source_target_pairs={{0,2},{1,3},{2,4},{3,5},{4,6},{5,7},{6,8},{7,9},{8,10},{9,11},{10,... | collective-permute-start | bytes 196616 | tf_op jit(solution)/shard_map/ppermute | solution.py:30
  231.8 3.2 %collective-permute-start.11 = (f32[1,128,128]{2,1,0:T(8,128)S(1)}, f32[1,128,128]{2,1,0:T(8,128)S(1)}, u32[]{:S(2)}, u32[]{:S(2)}) collective-permute-start(f32[1,128,128]{2,1,0:T(8,128)S(1)} %get-tuple-element.17), channel_id=1, source_target_pairs={{0,29},{1,30},{2,31},{3,0},{4,1},{5,2},{6,3},{7,4},{8,5},{9,6},{10... | collective-permute-start | bytes 196616 | tf_op jit(solution)/shard_map/ppermute | solution.py:30
  235.0 5.9 %collective-permute-start.13 = (f32[1,128,128]{2,1,0:T(8,128)S(1)}, f32[1,128,128]{2,1,0:T(8,128)S(1)}, u32[]{:S(2)}, u32[]{:S(2)}) collective-permute-start(f32[1,128,128]{2,1,0:T(8,128)S(1)} %get-tuple-element.15), channel_id=1, source_target_pairs={{0,28},{1,29},{2,30},{3,31},{4,0},{5,1},{6,2},{7,3},{8,4},{9,5},{1... | collective-permute-start | bytes 196616 | tf_op jit(solution)/shard_map/ppermute | solution.py:30
  241.0 3.4 %collective-permute-start.15 = (f32[1,128,128]{2,1,0:T(8,128)S(1)}, f32[1,128,128]{2,1,0:T(8,128)S(1)}, u32[]{:S(2)}, u32[]{:S(2)}) collective-permute-start(f32[1,128,128]{2,1,0:T(8,128)S(1)} %get-tuple-element.13), channel_id=1, source_target_pairs={{0,27},{1,28},{2,29},{3,30},{4,31},{5,0},{6,1},{7,2},{8,3},{9,4},{... | collective-permute-start | bytes 196616 | tf_op jit(solution)/shard_map/ppermute | solution.py:30
  244.6 3.7 %collective-permute-start.17 = (f32[1,128,128]{2,1,0:T(8,128)S(1)}, f32[1,128,128]{2,1,0:T(8,128)S(1)}, u32[]{:S(2)}, u32[]{:S(2)}) collective-permute-start(f32[1,128,128]{2,1,0:T(8,128)S(1)} %get-tuple-element.11), channel_id=1, source_target_pairs={{0,26},{1,27},{2,28},{3,29},{4,30},{5,31},{6,0},{7,1},{8,2},{9,3},... | collective-permute-start | bytes 196616 | tf_op jit(solution)/shard_map/ppermute | solution.py:30
  248.4 1.7 collective-permute-start.18
  250.2 10.8 %collective-permute-start.19 = (f32[1,128,128]{2,1,0:T(8,128)S(1)}, f32[1,128,128]{2,1,0:T(8,128)S(1)}, u32[]{:S(2)}, u32[]{:S(2)}) collective-permute-start(f32[1,128,128]{2,1,0:T(8,128)S(1)} %get-tuple-element.9), channel_id=1, source_target_pairs={{0,25},{1,26},{2,27},{3,28},{4,29},{5,30},{6,31},{7,0},{8,1},{9,2}... | collective-permute-start | bytes 196616 | tf_op jit(solution)/shard_map/ppermute | solution.py:30
  261.1 3.0 %collective-permute-start.21 = (f32[1,128,128]{2,1,0:T(8,128)S(1)}, f32[1,128,128]{2,1,0:T(8,128)S(1)}, u32[]{:S(2)}, u32[]{:S(2)}) collective-permute-start(f32[1,128,128]{2,1,0:T(8,128)S(1)} %get-tuple-element.7), channel_id=1, source_target_pairs={{0,16},{1,17},{2,18},{3,19},{4,20},{5,21},{6,22},{7,23},{8,24},{9,... | collective-permute-start | bytes 196616 | tf_op jit(solution)/shard_map/ppermute | solution.py:30
  264.2 5.5 %collective-permute-done.20 = f32[1,128,128]{2,1,0:T(8,128)S(1)} collective-permute-done((f32[1,128,128]{2,1,0:T(8,128)S(1)}, f32[1,128,128]{2,1,0:T(8,128)S(1)}, u32[]{:S(2)}, u32[]{:S(2)}) %collective-permute-start.20) | collective-permute-done | bytes 65568 | tf_op jit(solution)/shard_map/ppermute | solution.py:30
  269.7 1.0 copy-done.1
  (84 shorter events, 11.4 us)
Async XLA Ops:
  6.5 143.2 %all-gather.4.cloned.1.call-start = ((), (), s32[]{:S(2)}) async-start(), calls=%async_computation | async-start | bytes 17301504 | tf_op jit(solution)/shard_map/all_gather | solution.py:68
  7.3 197.2 %all-gather.6.cloned.1.call-start = ((), (), s32[]{:S(2)}) async-start(), calls=%async_computation.1 | async-start | bytes 4718592 | tf_op jit(solution)/shard_map/all_gather | solution.py:77
  7.3 10.0 %collective-permute-start = (bf16[1,16,128,128]{3,2,1,0:T(8,128)(2,1)}, bf16[1,16,128,128]{3,2,1,0:T(8,128)(2,1)S(1)}, u32[]{:S(2)}, u32[]{:S(2)}) collective-permute-start(bf16[1,16,128,128]{3,2,1,0:T(8,128)(2,1)} %param.4), channel_id=1, source_target_pairs={{0,32},{32,64},{64,96},{96,128},{128,160},{160,192},{192,224},{224... | collective-permute-start | bytes 1572872 | tf_op jit(solution)/shard_map/ppermute | solution.py:16
  7.3 10.1 %collective-permute-start.1 = (bf16[1,16,128,128]{3,2,1,0:T(8,128)(2,1)}, bf16[1,16,128,128]{3,2,1,0:T(8,128)(2,1)S(1)}, u32[]{:S(2)}, u32[]{:S(2)}) collective-permute-start(bf16[1,16,128,128]{3,2,1,0:T(8,128)(2,1)} %param.4), channel_id=1, source_target_pairs={{0,224},{32,0},{64,32},{96,64},{128,96},{160,128},{192,160},{224,1... | collective-permute-start | bytes 1572872 | tf_op jit(solution)/shard_map/ppermute | solution.py:21
  17.3 9.8 %collective-permute-start.2 = (bf16[1,16,128,128]{3,2,1,0:T(8,128)(2,1)S(1)}, bf16[1,16,128,128]{3,2,1,0:T(8,128)(2,1)S(1)}, u32[]{:S(2)}, u32[]{:S(2)}) collective-permute-start(bf16[1,16,128,128]{3,2,1,0:T(8,128)(2,1)S(1)} %collective-permute-done), channel_id=1, source_target_pairs={{0,32},{32,64},{64,96},{96,128},{128,160},{160,192},{192,224},{224... | collective-permute-start | bytes 1572872 | tf_op jit(solution)/shard_map/ppermute | solution.py:16
  17.5 15.1 %collective-permute-start.3 = (bf16[1,16,128,128]{3,2,1,0:T(8,128)(2,1)S(1)}, bf16[1,16,128,128]{3,2,1,0:T(8,128)(2,1)S(1)}, u32[]{:S(2)}, u32[]{:S(2)}) collective-permute-start(bf16[1,16,128,128]{3,2,1,0:T(8,128)(2,1)S(1)} %collective-permute-done.1), channel_id=1, source_target_pairs={{0,224},{32,0},{64,32},{96,64},{128,96},{160,128},{192,160},{224,1... | collective-permute-start | bytes 1572872 | tf_op jit(solution)/shard_map/ppermute | solution.py:21
  27.2 9.8 %collective-permute-start.4 = (bf16[1,16,128,128]{3,2,1,0:T(8,128)(2,1)S(1)}, bf16[1,16,128,128]{3,2,1,0:T(8,128)(2,1)S(1)}, u32[]{:S(2)}, u32[]{:S(2)}) collective-permute-start(bf16[1,16,128,128]{3,2,1,0:T(8,128)(2,1)S(1)} %collective-permute-done.2), channel_id=1, source_target_pairs={{0,32},{32,64},{64,96},{96,128},{128,160},{160,192},{192,224},{224... | collective-permute-start | bytes 1572872 | tf_op jit(solution)/shard_map/ppermute | solution.py:16
  32.6 9.6 %collective-permute-start.5 = (bf16[1,16,128,128]{3,2,1,0:T(8,128)(2,1)S(1)}, bf16[1,16,128,128]{3,2,1,0:T(8,128)(2,1)S(1)}, u32[]{:S(2)}, u32[]{:S(2)}) collective-permute-start(bf16[1,16,128,128]{3,2,1,0:T(8,128)(2,1)S(1)} %collective-permute-done.3), channel_id=1, source_target_pairs={{0,224},{32,0},{64,32},{96,64},{128,96},{160,128},{192,160},{224,1... | collective-permute-start | bytes 1572872 | tf_op jit(solution)/shard_map/ppermute | solution.py:21
  37.0 9.8 %collective-permute-start.6 = (bf16[1,16,128,128]{3,2,1,0:T(8,128)(2,1)S(1)}, bf16[1,16,128,128]{3,2,1,0:T(8,128)(2,1)S(1)}, u32[]{:S(2)}, u32[]{:S(2)}) collective-permute-start(bf16[1,16,128,128]{3,2,1,0:T(8,128)(2,1)S(1)} %collective-permute-done.4), channel_id=1, source_target_pairs={{0,32},{32,64},{64,96},{96,128},{128,160},{160,192},{192,224},{224... | collective-permute-start | bytes 1572872 | tf_op jit(solution)/shard_map/ppermute | solution.py:16
  160.3 9.1 %copy-start = (s32[16]{0:T(128)S(1)}, s32[16]{0:T(128)}, u32[]{:S(2)}) copy-start(s32[16]{0:T(128)} %constant.163.clone) | copy-start | bytes 196
  225.1 9.9 %collective-permute-start.7 = (f32[1,128,128]{2,1,0:T(8,128)S(1)}, f32[1,128,128]{2,1,0:T(8,128)S(1)}, u32[]{:S(2)}, u32[]{:S(2)}) collective-permute-start(f32[1,128,128]{2,1,0:T(8,128)S(1)} %get-tuple-element.21), channel_id=1, source_target_pairs={{0,31},{1,0},{2,1},{3,2},{4,3},{5,4},{6,5},{7,6},{8,7},{9,8},{10,9... | collective-permute-start | bytes 196616 | tf_op jit(solution)/shard_map/ppermute | solution.py:30
  225.9 9.1 %collective-permute-start.8 = (f32[1,128,128]{2,1,0:T(8,128)S(1)}, f32[1,128,128]{2,1,0:T(8,128)S(1)}, u32[]{:S(2)}, u32[]{:S(2)}) collective-permute-start(f32[1,128,128]{2,1,0:T(8,128)S(1)} %get-tuple-element.20), channel_id=1, source_target_pairs={{0,1},{1,2},{2,3},{3,4},{4,5},{5,6},{6,7},{7,8},{8,9},{9,10},{10,1... | collective-permute-start | bytes 196616 | tf_op jit(solution)/shard_map/ppermute | solution.py:30
  227.4 13.5 %collective-permute-start.9 = (f32[1,128,128]{2,1,0:T(8,128)S(1)}, f32[1,128,128]{2,1,0:T(8,128)S(1)}, u32[]{:S(2)}, u32[]{:S(2)}) collective-permute-start(f32[1,128,128]{2,1,0:T(8,128)S(1)} %get-tuple-element.19), channel_id=1, source_target_pairs={{0,30},{1,31},{2,0},{3,1},{4,2},{5,3},{6,4},{7,5},{8,6},{9,7},{10,... | collective-permute-start | bytes 196616 | tf_op jit(solution)/shard_map/ppermute | solution.py:30
  228.6 12.4 %collective-permute-start.10 = (f32[1,128,128]{2,1,0:T(8,128)S(1)}, f32[1,128,128]{2,1,0:T(8,128)S(1)}, u32[]{:S(2)}, u32[]{:S(2)}) collective-permute-start(f32[1,128,128]{2,1,0:T(8,128)S(1)} %get-tuple-element.18), channel_id=1, source_target_pairs={{0,2},{1,3},{2,4},{3,5},{4,6},{5,7},{6,8},{7,9},{8,10},{9,11},{10,... | collective-permute-start | bytes 196616 | tf_op jit(solution)/shard_map/ppermute | solution.py:30
  231.8 12.6 %collective-permute-start.11 = (f32[1,128,128]{2,1,0:T(8,128)S(1)}, f32[1,128,128]{2,1,0:T(8,128)S(1)}, u32[]{:S(2)}, u32[]{:S(2)}) collective-permute-start(f32[1,128,128]{2,1,0:T(8,128)S(1)} %get-tuple-element.17), channel_id=1, source_target_pairs={{0,29},{1,30},{2,31},{3,0},{4,1},{5,2},{6,3},{7,4},{8,5},{9,6},{10... | collective-permute-start | bytes 196616 | tf_op jit(solution)/shard_map/ppermute | solution.py:30
  235.0 9.6 %collective-permute-start.12 = (f32[1,128,128]{2,1,0:T(8,128)S(1)}, f32[1,128,128]{2,1,0:T(8,128)S(1)}, u32[]{:S(2)}, u32[]{:S(2)}) collective-permute-start(f32[1,128,128]{2,1,0:T(8,128)S(1)} %get-tuple-element.16), channel_id=1, source_target_pairs={{0,3},{1,4},{2,5},{3,6},{4,7},{5,8},{6,9},{7,10},{8,11},{9,12},{10... | collective-permute-start | bytes 196616 | tf_op jit(solution)/shard_map/ppermute | solution.py:30
  235.0 13.4 %collective-permute-start.13 = (f32[1,128,128]{2,1,0:T(8,128)S(1)}, f32[1,128,128]{2,1,0:T(8,128)S(1)}, u32[]{:S(2)}, u32[]{:S(2)}) collective-permute-start(f32[1,128,128]{2,1,0:T(8,128)S(1)} %get-tuple-element.15), channel_id=1, source_target_pairs={{0,28},{1,29},{2,30},{3,31},{4,0},{5,1},{6,2},{7,3},{8,4},{9,5},{1... | collective-permute-start | bytes 196616 | tf_op jit(solution)/shard_map/ppermute | solution.py:30
  240.9 9.3 %collective-permute-start.14 = (f32[1,128,128]{2,1,0:T(8,128)S(1)}, f32[1,128,128]{2,1,0:T(8,128)S(1)}, u32[]{:S(2)}, u32[]{:S(2)}) collective-permute-start(f32[1,128,128]{2,1,0:T(8,128)S(1)} %get-tuple-element.14), channel_id=1, source_target_pairs={{0,4},{1,5},{2,6},{3,7},{4,8},{5,9},{6,10},{7,11},{8,12},{9,13},{1... | collective-permute-start | bytes 196616 | tf_op jit(solution)/shard_map/ppermute | solution.py:30
  241.0 20.0 %collective-permute-start.15 = (f32[1,128,128]{2,1,0:T(8,128)S(1)}, f32[1,128,128]{2,1,0:T(8,128)S(1)}, u32[]{:S(2)}, u32[]{:S(2)}) collective-permute-start(f32[1,128,128]{2,1,0:T(8,128)S(1)} %get-tuple-element.13), channel_id=1, source_target_pairs={{0,27},{1,28},{2,29},{3,30},{4,31},{5,0},{6,1},{7,2},{8,3},{9,4},{... | collective-permute-start | bytes 196616 | tf_op jit(solution)/shard_map/ppermute | solution.py:30
  244.5 16.6 %collective-permute-start.16 = (f32[1,128,128]{2,1,0:T(8,128)S(1)}, f32[1,128,128]{2,1,0:T(8,128)S(1)}, u32[]{:S(2)}, u32[]{:S(2)}) collective-permute-start(f32[1,128,128]{2,1,0:T(8,128)S(1)} %get-tuple-element.12), channel_id=1, source_target_pairs={{0,5},{1,6},{2,7},{3,8},{4,9},{5,10},{6,11},{7,12},{8,13},{9,14},{... | collective-permute-start | bytes 196616 | tf_op jit(solution)/shard_map/ppermute | solution.py:30
  244.6 19.5 %collective-permute-start.17 = (f32[1,128,128]{2,1,0:T(8,128)S(1)}, f32[1,128,128]{2,1,0:T(8,128)S(1)}, u32[]{:S(2)}, u32[]{:S(2)}) collective-permute-start(f32[1,128,128]{2,1,0:T(8,128)S(1)} %get-tuple-element.11), channel_id=1, source_target_pairs={{0,26},{1,27},{2,28},{3,29},{4,30},{5,31},{6,0},{7,1},{8,2},{9,3},... | collective-permute-start | bytes 196616 | tf_op jit(solution)/shard_map/ppermute | solution.py:30
  248.4 15.7 %collective-permute-start.18 = (f32[1,128,128]{2,1,0:T(8,128)S(1)}, f32[1,128,128]{2,1,0:T(8,128)S(1)}, u32[]{:S(2)}, u32[]{:S(2)}) collective-permute-start(f32[1,128,128]{2,1,0:T(8,128)S(1)} %get-tuple-element.10), channel_id=1, source_target_pairs={{0,6},{1,7},{2,8},{3,9},{4,10},{5,11},{6,12},{7,13},{8,14},{9,15},... | collective-permute-start | bytes 196616 | tf_op jit(solution)/shard_map/ppermute | solution.py:30
  250.2 14.0 %collective-permute-start.19 = (f32[1,128,128]{2,1,0:T(8,128)S(1)}, f32[1,128,128]{2,1,0:T(8,128)S(1)}, u32[]{:S(2)}, u32[]{:S(2)}) collective-permute-start(f32[1,128,128]{2,1,0:T(8,128)S(1)} %get-tuple-element.9), channel_id=1, source_target_pairs={{0,25},{1,26},{2,27},{3,28},{4,29},{5,30},{6,31},{7,0},{8,1},{9,2}... | collective-permute-start | bytes 196616 | tf_op jit(solution)/shard_map/ppermute | solution.py:30
  261.0 8.7 %collective-permute-start.20 = (f32[1,128,128]{2,1,0:T(8,128)S(1)}, f32[1,128,128]{2,1,0:T(8,128)S(1)}, u32[]{:S(2)}, u32[]{:S(2)}) collective-permute-start(f32[1,128,128]{2,1,0:T(8,128)S(1)} %get-tuple-element.8), channel_id=1, source_target_pairs={{0,7},{1,8},{2,9},{3,10},{4,11},{5,12},{6,13},{7,14},{8,15},{9,16}... | collective-permute-start | bytes 196616 | tf_op jit(solution)/shard_map/ppermute | solution.py:30
  261.1 8.6 %collective-permute-start.21 = (f32[1,128,128]{2,1,0:T(8,128)S(1)}, f32[1,128,128]{2,1,0:T(8,128)S(1)}, u32[]{:S(2)}, u32[]{:S(2)}) collective-permute-start(f32[1,128,128]{2,1,0:T(8,128)S(1)} %get-tuple-element.7), channel_id=1, source_target_pairs={{0,16},{1,17},{2,18},{3,19},{4,20},{5,21},{6,22},{7,23},{8,24},{9,... | collective-permute-start | bytes 196616 | tf_op jit(solution)/shard_map/ppermute | solution.py:30
  269.7 1.0 copy-start.1
Sparse Core Ops, SparseCore 0:
  9.9 139.7 all-gather.3
  169.4 35.0 all-gather.5
